TPU v7x, 32 devices: a whole 2x2x4 slice. The times are simulated.
32 devices in a mesh: group: 2 (over y), dev: 8 (over z, x), tp: 2 (over core).
Axes of the slice: x: 2, y: 2, z: 4, core: 2. Of those that a mesh axis runs over, the one named last changes fastest.
Arguments:
- prompt_activations: bfloat16 [4096, 8192], P(('group', 'dev')), parts along dimension 0, may hold values from -6 to 6
- key_matrix: bfloat16 [8192, 512], P('dev', 'tp'), may hold values from -0.0625 to 0.0625
- value_matrix: bfloat16 [8192, 512], P('dev', 'tp'), may hold values from -0.0625 to 0.0625
- adapter_down_keyvalue: bfloat16 [8192, 128], P('dev'), may hold values from -0.0625 to 0.0625
- adapter_up_key: bfloat16 [64, 512], P(None, 'tp'), may hold values from -1.5 to 1.5
- adapter_up_value: bfloat16 [64, 512], P(None, 'tp'), may hold values from -1.5 to 1.5
- request_adapter: int32 [16], P('group'), parts along dimension 0, may hold values from 0 to 3
- page_request: int32 [1024, 1], P('group'), parts along dimension 0, may hold values from 0 to 7; in each aligned block of 64 rows (0 to 63, 64 to 127, ...) at most 8 rows name the same one
- context_tokens: int32 [16], P('group'), parts along dimension 0, may hold values from 64 to 256
- step_query: bfloat16 [16, 4096], P(('group', 'dev'), 'tp'), parts along dimension 0, may hold values from -256 to 256
- step_key: bfloat16 [16, 512], P(('group', 'dev'), 'tp'), parts along dimension 0, may hold values from -6 to 6
- step_value: bfloat16 [16, 512], P(('group', 'dev'), 'tp'), parts along dimension 0, may hold values from -6 to 6
- stored_keys: bfloat16 [16, 256, 512], P(('group', 'dev'), None, 'tp'), parts along dimension 0, may hold values from -6 to 6
- stored_values: bfloat16 [16, 256, 512], P(('group', 'dev'), None, 'tp'), parts along dimension 0, may hold values from -6 to 6
- output_matrix: bfloat16 [4096, 8192], P('tp', 'dev'), may hold values from -0.09375 to 0.09375
- adapter_down_output: bfloat16 [4096, 64], P('tp'), may hold values from -0.09375 to 0.09375
- adapter_up_output: bfloat16 [64, 8192], P(None, 'dev'), may hold values from -1.5 to 1.5
Outputs:
- attended: bfloat16 [16, 8192], P('group', 'dev'), parts along dimension 0
There are 2 independent parts, one for each index of `group`. A program takes and returns all parts, laid end to end along the dimension named above; an argument that names none is the same for every part. Nothing has to cross between parts.
Inputs may be any that keep to these rules, and one draw needn't show every extreme that they name: `page_request`: among the pages of one device's prompt block (aligned blocks of 64 pages), no request owns more than 8; every request owns at least one page.
All inputs are finite; a program needn't handle non-finite values.
Results may differ from a plain program's by a relative error of at most 0.0086.
Values may be sent and summed in bfloat16 or wider, within the bound.
A program may use at most 64 MiB of HBM per device.

v0:
```python
import jax
import jax.numpy as jnp
from jax import lax
from jax.sharding import PartitionSpec as P

HEADS = 32
KV_HEADS = 4
HEAD = 128
LOW_RANK = 16
ADAPTER_COUNT = 4
PAGE = 4
adapter_scale = 1.0
rope_base = 500000.0


def rotate(key_rows, positions):
    row_count = key_rows.shape[0]
    blocks = key_rows.reshape(row_count, -1, HEAD)
    half_size = HEAD // 2
    exponent = jnp.arange(half_size, dtype=jnp.float32) * (2.0 / HEAD)
    frequency = jnp.exp(-jnp.log(jnp.float32(rope_base)) * exponent)
    angles = positions.astype(jnp.float32)[:, None] * frequency[None, :]
    cosine = jnp.cos(angles)[:, None, :]
    sine_part = jnp.sin(angles)[:, None, :]
    first_half = blocks[..., :half_size]
    second_half = blocks[..., half_size:]
    turned = jnp.concatenate(
        [
            first_half * cosine - second_half * sine_part,
            second_half * cosine + first_half * sine_part,
        ],
        axis=-1,
    )
    return turned.reshape(row_count, -1)


def owner_ranks(owners, row_total):
    onehot = (owners[:, None] == jnp.arange(row_total, dtype=jnp.int32)[None, :]).astype(jnp.int32)
    before = jnp.cumsum(onehot, axis=0) - onehot
    rank = jnp.sum(before * onehot, axis=1)
    return (onehot, rank)


def mask_columns(narrowed, adapter_list):
    column = jnp.arange(narrowed.shape[1], dtype=jnp.int32)
    owner = column % (ADAPTER_COUNT * LOW_RANK) // LOW_RANK
    return jnp.where(owner[None, :] == adapter_list[:, None], narrowed, jnp.zeros_like(narrowed))


def selected_narrow(activation_rows, adapter_down, adapter_list):
    narrowed = jnp.dot(activation_rows, adapter_down, preferred_element_type=jnp.float32)
    return mask_columns(narrowed, adapter_list)


def widened(selected_rows, up_key, up_value):
    split_at = ADAPTER_COUNT * LOW_RANK
    highest = lax.Precision.HIGHEST
    key_portion = jnp.dot(
        selected_rows[:, :split_at], up_key.astype(jnp.float32), precision=highest
    )
    value_portion = jnp.dot(
        selected_rows[:, split_at:], up_value.astype(jnp.float32), precision=highest
    )
    return (adapter_scale * key_portion, adapter_scale * value_portion)


def attend_local(
    query,
    old_keys,
    old_values,
    old_length,
    fresh_keys,
    fresh_values,
    fresh_valid,
    last_key,
    last_value,
):
    group_size = HEADS // KV_HEADS
    query_heads = query.reshape(-1, group_size, HEAD)
    kv_local = query_heads.shape[0]
    scale_factor = HEAD ** (-0.5)

    def score_of(key_rows):
        shaped = key_rows.reshape(key_rows.shape[0], kv_local, HEAD)
        return (
            jnp.einsum("kgd,lkd->kgl", query_heads, shaped, preferred_element_type=jnp.float32)
            * scale_factor
        )

    def mix_with(probs, value_rows):
        shaped = value_rows.reshape(value_rows.shape[0], kv_local, HEAD)
        return jnp.einsum("kgl,lkd->kgd", probs, shaped, preferred_element_type=jnp.float32)

    old_valid = jnp.arange(old_keys.shape[0], dtype=jnp.int32) < old_length
    old_scores = jnp.where(old_valid[None, None, :], score_of(old_keys), -1e30)
    fresh_scores = jnp.where(fresh_valid[None, None, :], score_of(fresh_keys), -1e30)
    last_score = score_of(last_key[None, :])
    top = jnp.maximum(
        jnp.maximum(
            jnp.max(old_scores, axis=-1, keepdims=True),
            jnp.max(fresh_scores, axis=-1, keepdims=True),
        ),
        last_score,
    )
    old_weights = jnp.exp(old_scores - top)
    fresh_weights = jnp.exp(fresh_scores - top)
    last_weight = jnp.exp(last_score - top)
    total = (
        jnp.sum(old_weights, axis=-1, keepdims=True)
        + jnp.sum(fresh_weights, axis=-1, keepdims=True)
        + last_weight
    )
    output = mix_with((old_weights / total).astype(jnp.bfloat16), old_values)
    output = output + mix_with((fresh_weights / total).astype(jnp.bfloat16), fresh_values)
    output = output + mix_with((last_weight / total).astype(jnp.bfloat16), last_value[None, :])
    return output.reshape(-1).astype(jnp.bfloat16)


def per_device(
    prompt_activations,
    key_matrix,
    value_matrix,
    adapter_down_keyvalue,
    adapter_up_key,
    adapter_up_value,
    request_adapter,
    page_request,
    context_tokens,
    step_query,
    step_key,
    step_value,
    stored_keys,
    stored_values,
    output_matrix,
    adapter_down_output,
    adapter_up_output,
):
    devices = lax.axis_size("dev")
    device = lax.axis_index("dev")
    tok_count = prompt_activations.shape[0]
    pages_here = tok_count // PAGE
    capacity = max(2, (pages_here + devices - 1) // devices)
    row_total = request_adapter.shape[0]
    owners = page_request[:, 0]
    onehot, rank = owner_ranks(owners, row_total)
    first_page = device * pages_here
    my_owners = lax.dynamic_slice_in_dim(owners, first_page, pages_here, 0)
    my_rank = lax.dynamic_slice_in_dim(rank, first_page, pages_here, 0)
    tokens = jnp.arange(tok_count, dtype=jnp.int32)
    token_page = tokens // PAGE
    token_owner = jnp.take(my_owners, token_page)
    position = (
        jnp.take(context_tokens, token_owner) + jnp.take(my_rank, token_page) * PAGE + tokens % PAGE
    )
    adapter_list = jnp.take(request_adapter, token_owner)
    key_width = key_matrix.shape[1]

    def add_rows(portion):
        return jnp.dot(prompt_activations, portion, preferred_element_type=jnp.float32)

    key_raw = add_rows(lax.all_gather(key_matrix, "dev", axis=0, tiled=True))
    value_raw = add_rows(lax.all_gather(value_matrix, "dev", axis=0, tiled=True))
    down_complete = lax.all_gather(adapter_down_keyvalue, "dev", axis=0, tiled=True)
    narrowed = jnp.dot(prompt_activations, down_complete, preferred_element_type=jnp.float32)
    selected_rows = mask_columns(narrowed, adapter_list)
    key_delta, value_delta = widened(selected_rows, adapter_up_key, adapter_up_value)
    key_rows = rotate(key_raw + key_delta, position).astype(jnp.bfloat16)
    value_rows = (value_raw + value_delta).astype(jnp.bfloat16)
    joined_rows = jnp.concatenate([key_rows, value_rows], axis=1)
    local_hot = (my_owners[:, None] == jnp.arange(row_total, dtype=jnp.int32)[None, :]).astype(
        jnp.int32
    )
    local_before = jnp.cumsum(local_hot, axis=0) - local_hot
    local_slot = jnp.sum(local_before * local_hot, axis=1)
    peer_slots = capacity * PAGE
    target = token_owner * peer_slots + jnp.take(local_slot, token_page) * PAGE + tokens % PAGE
    outgoing = (
        jnp.zeros((devices * peer_slots, 2 * key_width), jnp.bfloat16).at[target].set(joined_rows)
    )
    outgoing = outgoing.reshape(devices, peer_slots, 2 * key_width)
    incoming = lax.all_to_all(outgoing, "dev", split_axis=0, concat_axis=0, tiled=True)
    fresh_keys = incoming[:, :, :key_width].reshape(-1, key_width)
    fresh_values = incoming[:, :, key_width:].reshape(-1, key_width)
    my_column = jnp.take(onehot, device, axis=1)
    count_from = jnp.sum(my_column.reshape(devices, pages_here), axis=1)
    slot_page = jnp.arange(peer_slots, dtype=jnp.int32) // PAGE
    fresh_valid = (slot_page[None, :] < count_from[:, None]).reshape(-1)
    mixed_local = attend_local(
        step_query[0],
        stored_keys[0],
        stored_values[0],
        jnp.take(context_tokens, device),
        fresh_keys,
        fresh_values,
        fresh_valid,
        step_key[0],
        step_value[0],
    ).reshape(1, -1)
    portion = lax.all_gather(mixed_local, "dev", axis=0, tiled=True)
    plain_result = jnp.dot(portion, output_matrix, preferred_element_type=jnp.float32)
    selected_output = selected_narrow(portion, adapter_down_output, request_adapter)
    partial_output = plain_result + adapter_scale * jnp.dot(
        selected_output, adapter_up_output.astype(jnp.float32), precision=lax.Precision.HIGHEST
    )
    return lax.psum(partial_output, "tp").astype(jnp.bfloat16)


def solution(mesh):
    return jax.shard_map(
        per_device,
        mesh=mesh,
        in_specs=(
            P(("group", "dev"), None),
            P("dev", "tp"),
            P("dev", "tp"),
            P("dev", None),
            P(None, "tp"),
            P(None, "tp"),
            P("group"),
            P("group", None),
            P("group"),
            P(("group", "dev"), "tp"),
            P(("group", "dev"), "tp"),
            P(("group", "dev"), "tp"),
            P(("group", "dev"), None, "tp"),
            P(("group", "dev"), None, "tp"),
            P("tp", "dev"),
            P("tp", None),
            P(None, "dev"),
        ),
        out_specs=P("group", "dev"),
        check_vma=False,
    )
```

profile of v0, /device:TPU:0, one launch (start us, length us, event | category | flops | bytes accessed | tf_op | source)
XLA Modules:
  0.0 273.4 jit_solution(10275499087581960177)
XLA Ops:
  6.5 0.7 all-gather.7.cloned.1.call-update
  7.3 0.7 all-gather.9.cloned.1.call-update
  8.0 0.0 all-gather.5.cloned.1.call-start
  8.1 0.7 all-gather.5.cloned.1.call-update
  8.8 0.7 fusion.22
  9.4 1.1 reduce-window.6
  10.6 0.2 slice_reduce_fusion
  10.8 0.8 fusion.20
  11.6 0.1 dynamic_slice.10
  11.7 0.7 dynamic-slice_bitcast_fusion
  12.4 1.9 gather_fusion
  14.3 1.9 gather_fusion.2
  16.2 0.7 fusion.21
  16.9 0.1 select_n.127
  17.0 0.1 reduce_sum.45
  17.1 0.1 fusion.18
  17.2 0.1 reduce_window_sum.26
  17.3 0.2 select_reduce_fusion
  17.4 1.9 gather_fusion.1
  19.3 0.7 fusion.46
  20.6 0.7 fusion.47
  21.3 0.1 broadcast_compare_fusion
  21.4 9.7 %fusion.41 = (f32[256]{0:T(256)S(1)}, s32[256]{0:T(256)S(1)}, s32[256]{0:T(256)S(1)}) fusion(s32[256]{0:T(256)S(1)} %gather_fusion.2, s32[]{:T(128)} %bitcast.19, s32[]{:T(128)} %bitcast.18, s32[]{:T(128)} %bitcast.17, s32[]{:T(128)} %bitcast.16, s32[]{:T(128)} %bitcast.15, s32[]{:T(128)} %bitcast.14, s32[]{:T(128)} %bitcast.13, s32[]{:T(128)} %bitcast.12, ...), kind=kLoop, calls=%fused_computation.94 | loop fusion | flops 15616 | bytes 6208 | tf_op jit(solution)/shard_map/convert_element_type | solution.py:22
  31.1 0.3 multiply_cosine_fusion
  31.4 29.8 %all-gather.7.cloned.1.call-done = bf16[8192,128]{1,0:T(8,128)(2,1)} async-done(((bf16[1024,128]{1,0:T(8,128)(2,1)}), bf16[8192,128]{1,0:T(8,128)(2,1)}) %all-gather.7.cloned.1.call-update) | async-done | bytes 2097168 | tf_op jit(solution)/shard_map/all_gather | solution.py:163
  61.3 4.4 %convolution_select_fusion = f32[256,128]{0,1:T(8,128)S(1)} fusion(bf16[256,8192]{1,0:T(8,128)(2,1)} %param.21, bf16[8192,128]{1,0:T(8,128)(2,1)} %all-gather.7.cloned.1.call-done, s32[256]{0:T(256)S(1)} %get-tuple-element.40, s32[128]{0:T(128)S(1)} %and_select_fusion.2), kind=kOutput, calls=%fused_computation.7 | convolution fusion | flops 536936448 | bytes 6424064 | tf_op jit(solution)/shard_map/dot_general | solution.py:164
  65.6 69.1 %all-gather.9.cloned.1.call-done = bf16[8192,256]{1,0:T(8,128)(2,1)} async-done(((bf16[1024,256]{1,0:T(8,128)(2,1)}), bf16[8192,256]{1,0:T(8,128)(2,1)}) %all-gather.9.cloned.1.call-update) | async-done | bytes 4194320 | tf_op jit(solution)/shard_map/all_gather | solution.py:162
  134.7 5.2 %fusion.51 = f32[256,256]{0,1:T(8,128)S(1)} fusion(bf16[256,8192]{1,0:T(8,128)(2,1)} %param.21, bf16[8192,256]{1,0:T(8,128)(2,1)} %all-gather.9.cloned.1.call-done), kind=kOutput, calls=%fused_computation.123 | convolution fusion | flops 1073741824 | bytes 8650752 | tf_op jit(solution)/shard_map/dot_general | solution.py:159
  139.9 0.3 fusion
  140.3 67.9 %all-gather.5.cloned.1.call-done = bf16[8192,256]{1,0:T(8,128)(2,1)} async-done(((bf16[1024,256]{1,0:T(8,128)(2,1)}), bf16[8192,256]{1,0:T(8,128)(2,1)}) %all-gather.5.cloned.1.call-update) | async-done | bytes 4194320 | tf_op jit(solution)/shard_map/all_gather | solution.py:161
  208.2 5.2 %fusion.50 = f32[256,256]{0,1:T(8,128)S(1)} fusion(bf16[256,8192]{1,0:T(8,128)(2,1)} %param.21, bf16[8192,256]{1,0:T(8,128)(2,1)} %all-gather.5.cloned.1.call-done), kind=kOutput, calls=%fused_computation.122 | convolution fusion | flops 1073741824 | bytes 8650752 | tf_op jit(solution)/shard_map/dot_general | solution.py:159
  213.5 0.3 convolution_add_fusion.1
  213.9 0.1 copy.27
  214.0 2.2 scatter_custom_fusion
  216.2 3.4 %all-to-all-start = ((bf16[8,32,512]{2,1,0:T(8,128)(2,1)}), bf16[8,32,512]{2,1,0:T(8,128)(2,1)S(1)}, u32[]{:S(2)}, u32[]{:S(2)}) async-start(bf16[8,32,512]{2,1,0:T(8,128)(2,1)} %bitcast.24), calls=%async_computation | async-start | bytes 524288 | tf_op jit(solution)/shard_map/all_to_all | solution.py:181
  219.6 0.1 lt.84
  219.9 0.1 fusion.31
  220.0 0.2 fusion.48
  220.2 8.0 %all-to-all-done = bf16[8,32,512]{2,1,0:T(8,128)(2,1)S(1)} async-done(((bf16[8,32,512]{2,1,0:T(8,128)(2,1)}), bf16[8,32,512]{2,1,0:T(8,128)(2,1)S(1)}, u32[]{:S(2)}, u32[]{:S(2)}) %all-to-all-start) | async-done | bytes 262176 | tf_op jit(solution)/shard_map/all_to_all | solution.py:181
  228.3 0.2 fusion.49
  228.6 0.2 fusion.24
  228.7 0.2 fusion.7
  228.9 0.2 fusion.5
  229.2 30.5 %all-gather = bf16[8,1,2048]{2,1,0:T(2,128)(2,1)S(1)} all-gather(bf16[1,1,2048]{2,1,0:T(2,128)(2,1)S(1)} %reshape.342), channel_id=1, replica_groups=mesh['group'=2,'dev'=8,'tp'=2] {'dev'}, dimensions={0}, use_global_device_ids=true | all-gather | bytes 36864 | tf_op jit(solution)/shard_map/all_gather | solution.py:199
  259.7 2.8 %fusion.16 = f32[8,1024]{1,0:T(8,128)S(1)} fusion(bf16[2048,1024]{1,0:T(8,128)(2,1)} %param.35, bf16[8,1,2048]{2,1,0:T(2,128)(2,1)S(1)} %all-gather), kind=kOutput, calls=%fused_computation.34 | convolution fusion | flops 33554432 | bytes 4259840 | tf_op jit(solution)/shard_map/dot_general | solution.py:200
  262.5 0.2 convolution_select_fusion.1
  262.7 0.2 convolution_add_fusion.2
  262.9 4.0 %psum.7 = bf16[8,1024]{1,0:T(8,128)(2,1)} all-reduce(f32[8,1024]{1,0:T(8,128)S(1)} %convolution_add_fusion.2), channel_id=1, replica_groups=mesh['group'=2,'dev'=8,'tp'=2] {'tp'}, use_global_device_ids=true, to_apply=%region_11.14 | all-reduce | flops 8192 | bytes 49152 | tf_op jit(solution)/shard_map/psum | solution.py:205
  (47 shorter events, 0.5 us)
Async XLA Ops:
  6.5 256.0 %copy-start = (bf16[2048,64]{0,1:T(8,128)(2,1)S(1)}, bf16[2048,64]{0,1:T(8,128)(2,1)}, u32[]{:S(2)}) copy-start(bf16[2048,64]{0,1:T(8,128)(2,1)} %param.36) | copy-start | bytes 786436
  6.5 12.8 %copy-start.4 = (s32[8]{0:T(128)S(1)}, s32[8]{0:T(128)}, u32[]{:S(2)}) copy-start(s32[8]{0:T(128)} %param.29) | copy-start | bytes 100
  6.5 14.1 %copy-start.6 = (s32[8]{0:T(128)S(1)}, s32[8]{0:T(128)}, u32[]{:S(2)}) copy-start(s32[8]{0:T(128)} %param.27) | copy-start | bytes 100
  6.5 54.7 %all-gather.7.cloned.1.call-start = ((), (), s32[]{:S(2)}) async-start(), calls=%async_computation.2 | async-start | bytes 2359296 | tf_op jit(solution)/shard_map/all_gather | solution.py:163
  7.3 127.5 %all-gather.9.cloned.1.call-start = ((), (), s32[]{:S(2)}) async-start(), calls=%async_computation.3 | async-start | bytes 4718592 | tf_op jit(solution)/shard_map/all_gather | solution.py:162
  8.0 200.2 %all-gather.5.cloned.1.call-start = ((), (), s32[]{:S(2)}) async-start(), calls=%async_computation.1 | async-start | bytes 4718592 | tf_op jit(solution)/shard_map/all_gather | solution.py:161
  65.6 74.3 %copy-start.7 = (bf16[64,256]{1,0:T(8,128)(2,1)S(1)}, bf16[64,256]{1,0:T(8,128)(2,1)}, u32[]{:S(2)}) copy-start(bf16[64,256]{1,0:T(8,128)(2,1)} %param.26) | copy-start | bytes 98308
  140.3 73.2 %copy-start.5 = (bf16[64,256]{1,0:T(8,128)(2,1)S(1)}, bf16[64,256]{1,0:T(8,128)(2,1)}, u32[]{:S(2)}) copy-start(bf16[64,256]{1,0:T(8,128)(2,1)} %param.25) | copy-start | bytes 98308
  140.3 79.3 %copy-start.9 = (bf16[1,256]{1,0:T(2,128)(2,1)S(1)}, bf16[1,256]{1,0:T(2,128)(2,1)}, u32[]{:S(2)}) copy-start(bf16[1,256]{1,0:T(2,128)(2,1)} %param.32) | copy-start | bytes 1540
  140.3 79.4 %copy-start.1 = (bf16[1,256,256]{2,1,0:T(8,128)(2,1)S(1)}, bf16[1,256,256]{2,1,0:T(8,128)(2,1)}, u32[]{:S(2)}) copy-start(bf16[1,256,256]{2,1,0:T(8,128)(2,1)} %param.33) | copy-start | bytes 393220
  140.3 79.5 %copy-start.2 = (bf16[1,256,256]{2,1,0:T(8,128)(2,1)S(1)}, bf16[1,256,256]{2,1,0:T(8,128)(2,1)}, u32[]{:S(2)}) copy-start(bf16[1,256,256]{2,1,0:T(8,128)(2,1)} %param.34) | copy-start | bytes 393220
  140.3 79.5 %copy-start.8 = (bf16[1,2048]{1,0:T(2,128)(2,1)S(1)}, bf16[1,2048]{1,0:T(2,128)(2,1)}, u32[]{:S(2)}) copy-start(bf16[1,2048]{1,0:T(2,128)(2,1)} %param.30) | copy-start | bytes 12292
  140.3 79.5 %copy-start.10 = (bf16[1,256]{1,0:T(2,128)(2,1)S(1)}, bf16[1,256]{1,0:T(2,128)(2,1)}, u32[]{:S(2)}) copy-start(bf16[1,256]{1,0:T(2,128)(2,1)} %param.31) | copy-start | bytes 1540
  213.9 48.9 %copy-start.3 = (bf16[64,1024]{1,0:T(8,128)(2,1)S(1)}, bf16[64,1024]{1,0:T(8,128)(2,1)}, u32[]{:S(2)}) copy-start(bf16[64,1024]{1,0:T(8,128)(2,1)} %param.37) | copy-start | bytes 393220
  216.2 12.0 %all-to-all-start = ((bf16[8,32,512]{2,1,0:T(8,128)(2,1)}), bf16[8,32,512]{2,1,0:T(8,128)(2,1)S(1)}, u32[]{:S(2)}, u32[]{:S(2)}) async-start(bf16[8,32,512]{2,1,0:T(8,128)(2,1)} %bitcast.24), calls=%async_computation | async-start | bytes 524288 | tf_op jit(solution)/shard_map/all_to_all | solution.py:181
Sparse Core Ops, SparseCore 0:
  9.5 51.7 all-gather.6
  63.4 71.3 all-gather.8
  136.9 71.3 all-gather.4
where the time goes:
time: 274 us; the launch traced here: 273 us
  waiting for transfers between devices  177 us (65%)
  blocking collectives  34.5 us (13%)
  matrix products  19.5 us (7%)
  other arithmetic  14.3 us (5%)
  between operations  14 us (5%)
  local copies, waits for them, and re-layouts  10.7 us (4%)
  starting transfers between devices  3.49 us (1%)
    all_gather x1, waiting for transfers between devices, per_device(): lax.all_gather(value_matrix, 'dev', axis=0, tiled=True)  69.1 us
    all_gather x1, waiting for transfers between devices, per_device(): key_raw = add_rows(lax.all_gather(key_matrix, 'dev', axis=0, tiled=True))  67.9 us
    all_gather x1, blocking collectives, per_device(): portion = lax.all_gather(mixed_local, 'dev', axis=0, tiled=True)  30.5 us
    all_gather x1, waiting for transfers between devices, per_device(): lax.all_gather(adapter_down_keyvalue, 'dev', axis=0, tiled=True)  29.8 us
    dot_general x2, matrix products, add_rows(): jnp.dot(prompt_activations, portion, preferred_element_type=jnp.float32)  10.4 us
    convert_element_type x1, other arithmetic, rotate(): angles = positions.astype(jnp.float32)[:, None] * frequency[None, :]  9.74 us
    all_to_all x1, waiting for transfers between devices, per_device(): lax.all_to_all(outgoing, 'dev', split_axis=0, concat_axis=0, tiled=True)  8 us
  transfers between devices with their start and end apart: 4, of which 4 were waited for; matrix products, arithmetic and copies ran while one was open for 12% of the time, Pallas kernels for 0%

commit v1 on v0

--- a/solution.py
+++ b/solution.py
@@ -196,7 +196,9 @@
         step_key[0],
         step_value[0],
     ).reshape(1, -1)
-    portion = lax.all_gather(mixed_local, "dev", axis=0, tiled=True)
+    portion = jnp.concatenate(
+        lax.all_to_all(jnp.stack([mixed_local] * lax.axis_size("dev")), "dev", 0, 0), axis=0
+    )
     plain_result = jnp.dot(portion, output_matrix, preferred_element_type=jnp.float32)
     selected_output = selected_narrow(portion, adapter_down_output, request_adapter)
     partial_output = plain_result + adapter_scale * jnp.dot(

time: 274 us -> 256 us (0.934)
  blocking collectives: 34.5 us -> 3.99 us
  waiting for transfers between devices: 177 us -> 184 us
  starting transfers between devices: 3.49 us -> 7.08 us
    all_gather x1 -> x0, blocking collectives: 30.5 us -> none  [per_device(): portion = lax.all_gather(mixed_local, 'dev', axis=0, tiled=True)]
    all_to_all x0 -> x1, waiting for transfers between devices: none -> 6.68 us  [per_device(): lax.all_to_all(jnp.stack([mixed_local] * lax.axis_size('dev')), 'dev', 0, 0)]
    all_to_all x0 -> x1, starting transfers between devices: none -> 3.59 us  [per_device(): lax.all_to_all(jnp.stack([mixed_local] * lax.axis_size('dev')), 'dev', 0, 0)]
  transfers between devices with their start and end apart: 4 -> 5, of which waited for: 4 -> 5; matrix products, arithmetic and copies ran while one was open for 12% -> 13% of each run, Pallas kernels for 0% -> 0%
where the time goes in v1:
time: 256 us; the launch traced here: 255 us
  waiting for transfers between devices  184 us (72%)
  matrix products  19.5 us (8%)
  other arithmetic  15.1 us (6%)
  between operations  14 us (5%)
  local copies, waits for them, and re-layouts  11.9 us (5%)
  starting transfers between devices  7.08 us (3%)
  blocking collectives  3.99 us (2%)
    all_gather x1, waiting for transfers between devices, per_device(): lax.all_gather(value_matrix, 'dev', axis=0, tiled=True)  69.1 us
    all_gather x1, waiting for transfers between devices, per_device(): key_raw = add_rows(lax.all_gather(key_matrix, 'dev', axis=0, tiled=True))  67.9 us
    all_gather x1, waiting for transfers between devices, per_device(): lax.all_gather(adapter_down_keyvalue, 'dev', axis=0, tiled=True)  29.8 us
    dot_general x2, matrix products, add_rows(): jnp.dot(prompt_activations, portion, preferred_element_type=jnp.float32)  10.4 us
    convert_element_type x1, other arithmetic, rotate(): angles = positions.astype(jnp.float32)[:, None] * frequency[None, :]  9.74 us
    all_to_all x1, waiting for transfers between devices, per_device(): lax.all_to_all(outgoing, 'dev', split_axis=0, concat_axis=0, tiled=True)  8 us
    all_to_all x1, waiting for transfers between devices, per_device(): lax.all_to_all(jnp.stack([mixed_local] * lax.axis_size('dev')), 'dev', 0, 0)  6.68 us
  transfers between devices with their start and end apart: 5, of which 5 were waited for; matrix products, arithmetic and copies ran while one was open for 13% of the time, Pallas kernels for 0%

profile of v1, /device:TPU:0, one launch (start us, length us, event | category | flops | bytes accessed | tf_op | source)
XLA Modules:
  0.0 255.2 jit_solution(1719473546504224651)
XLA Ops:
  6.5 0.7 all-gather.6.cloned.1.call-update
  7.3 0.7 all-gather.8.cloned.1.call-update
  8.1 0.7 all-gather.4.cloned.1.call-update
  8.8 0.7 fusion.23
  9.4 1.1 reduce-window.6
  10.6 0.2 slice_reduce_fusion
  10.8 0.8 fusion.21
  11.7 0.7 dynamic-slice_bitcast_fusion
  12.4 1.9 gather_fusion
  14.3 1.9 gather_fusion.2
  16.2 0.7 fusion.22
  16.9 0.1 select_n.127
  17.0 0.1 reduce_sum.45
  17.2 0.1 reduce_window_sum.26
  17.3 0.2 select_reduce_fusion
  17.4 1.9 gather_fusion.1
  19.3 0.7 fusion.47
  20.6 0.7 fusion.48
  21.4 9.7 %fusion.42 = (f32[256]{0:T(256)S(1)}, s32[256]{0:T(256)S(1)}, s32[256]{0:T(256)S(1)}) fusion(s32[256]{0:T(256)S(1)} %gather_fusion.2, s32[]{:T(128)} %bitcast.19, s32[]{:T(128)} %bitcast.18, s32[]{:T(128)} %bitcast.17, s32[]{:T(128)} %bitcast.16, s32[]{:T(128)} %bitcast.15, s32[]{:T(128)} %bitcast.14, s32[]{:T(128)} %bitcast.13, s32[]{:T(128)} %bitcast.12, ...), kind=kLoop, calls=%fused_computation.95 | loop fusion | flops 15616 | bytes 6208 | tf_op jit(solution)/shard_map/convert_element_type | solution.py:22
  31.1 0.3 multiply_cosine_fusion
  31.4 29.8 %all-gather.6.cloned.1.call-done = bf16[8192,128]{1,0:T(8,128)(2,1)} async-done(((bf16[1024,128]{1,0:T(8,128)(2,1)}), bf16[8192,128]{1,0:T(8,128)(2,1)}) %all-gather.6.cloned.1.call-update) | async-done | bytes 2097168 | tf_op jit(solution)/shard_map/all_gather | solution.py:163
  61.3 4.4 %convolution_select_fusion = f32[256,128]{0,1:T(8,128)S(1)} fusion(bf16[256,8192]{1,0:T(8,128)(2,1)} %param.21, bf16[8192,128]{1,0:T(8,128)(2,1)} %all-gather.6.cloned.1.call-done, s32[256]{0:T(256)S(1)} %get-tuple-element.40, s32[128]{0:T(128)S(1)} %and_select_fusion.2), kind=kOutput, calls=%fused_computation.7 | convolution fusion | flops 536936448 | bytes 6424064 | tf_op jit(solution)/shard_map/dot_general | solution.py:164
  65.6 69.1 %all-gather.8.cloned.1.call-done = bf16[8192,256]{1,0:T(8,128)(2,1)} async-done(((bf16[1024,256]{1,0:T(8,128)(2,1)}), bf16[8192,256]{1,0:T(8,128)(2,1)}) %all-gather.8.cloned.1.call-update) | async-done | bytes 4194320 | tf_op jit(solution)/shard_map/all_gather | solution.py:162
  134.7 5.2 %fusion.52 = f32[256,256]{0,1:T(8,128)S(1)} fusion(bf16[256,8192]{1,0:T(8,128)(2,1)} %param.21, bf16[8192,256]{1,0:T(8,128)(2,1)} %all-gather.8.cloned.1.call-done), kind=kOutput, calls=%fused_computation.124 | convolution fusion | flops 1073741824 | bytes 8650752 | tf_op jit(solution)/shard_map/dot_general | solution.py:159
  139.9 0.3 fusion
  140.3 67.9 %all-gather.4.cloned.1.call-done = bf16[8192,256]{1,0:T(8,128)(2,1)} async-done(((bf16[1024,256]{1,0:T(8,128)(2,1)}), bf16[8192,256]{1,0:T(8,128)(2,1)}) %all-gather.4.cloned.1.call-update) | async-done | bytes 4194320 | tf_op jit(solution)/shard_map/all_gather | solution.py:161
  208.2 5.2 %fusion.51 = f32[256,256]{0,1:T(8,128)S(1)} fusion(bf16[256,8192]{1,0:T(8,128)(2,1)} %param.21, bf16[8192,256]{1,0:T(8,128)(2,1)} %all-gather.4.cloned.1.call-done), kind=kOutput, calls=%fused_computation.123 | convolution fusion | flops 1073741824 | bytes 8650752 | tf_op jit(solution)/shard_map/dot_general | solution.py:159
  213.5 0.3 convolution_add_fusion.1
  213.9 0.1 copy.26
  214.0 2.2 scatter_custom_fusion
  216.2 3.4 %all-to-all-start = ((bf16[8,32,512]{2,1,0:T(8,128)(2,1)}), bf16[8,32,512]{2,1,0:T(8,128)(2,1)S(1)}, u32[]{:S(2)}, u32[]{:S(2)}) async-start(bf16[8,32,512]{2,1,0:T(8,128)(2,1)} %bitcast.24), calls=%async_computation | async-start | bytes 524288 | tf_op jit(solution)/shard_map/all_to_all | solution.py:181
  219.6 0.1 lt.84
  219.9 0.1 fusion.32
  220.0 0.2 fusion.49
  220.2 8.0 %all-to-all-done = bf16[8,32,512]{2,1,0:T(8,128)(2,1)S(1)} async-done(((bf16[8,32,512]{2,1,0:T(8,128)(2,1)}), bf16[8,32,512]{2,1,0:T(8,128)(2,1)S(1)}, u32[]{:S(2)}, u32[]{:S(2)}) %all-to-all-start) | async-done | bytes 262176 | tf_op jit(solution)/shard_map/all_to_all | solution.py:181
  228.3 0.2 fusion.50
  228.6 0.2 fusion.25
  228.7 0.2 fusion.8
  228.9 0.2 fusion.6
  229.2 0.5 broadcast.390
  229.7 0.8 reduce.7
  230.5 0.6 reshape.379
  231.2 3.6 %all-to-all-start.1 = ((bf16[8,2,1024]{2,1,0:T(2,128)(2,1)}), bf16[8,2,1024]{2,1,0:T(2,128)(2,1)S(1)}, u32[]{:S(2)}, u32[]{:S(2)}) async-start(bf16[8,2,1024]{2,1,0:T(2,128)(2,1)} %reshape.379), calls=%async_computation.1 | async-start | bytes 65536 | tf_op jit(solution)/shard_map/all_to_all | solution.py:200
  234.8 6.7 %all-to-all-done.1 = bf16[8,2,1024]{2,1,0:T(2,128)(2,1)S(1)} async-done(((bf16[8,2,1024]{2,1,0:T(2,128)(2,1)}), bf16[8,2,1024]{2,1,0:T(2,128)(2,1)S(1)}, u32[]{:S(2)}, u32[]{:S(2)}) %all-to-all-start.1) | async-done | bytes 32800 | tf_op jit(solution)/shard_map/all_to_all | solution.py:200
  241.5 2.8 %fusion.17 = f32[8,1024]{1,0:T(8,128)S(1)} fusion(bf16[2048,1024]{1,0:T(8,128)(2,1)} %param.35, bf16[8,1,2048]{2,1,0:T(2,128)(2,1)S(1)} %reshape.380), kind=kOutput, calls=%fused_computation.35 | convolution fusion | flops 33554432 | bytes 4259840 | tf_op jit(solution)/shard_map/dot_general | solution.py:202
  244.3 0.2 convolution_select_fusion.1
  244.5 0.2 convolution_add_fusion.2
  244.7 4.0 %psum.7 = bf16[8,1024]{1,0:T(8,128)(2,1)} all-reduce(f32[8,1024]{1,0:T(8,128)S(1)} %convolution_add_fusion.2), channel_id=1, replica_groups=mesh['group'=2,'dev'=8,'tp'=2] {'tp'}, use_global_device_ids=true, to_apply=%region_11.14 | all-reduce | flops 8192 | bytes 49152 | tf_op jit(solution)/shard_map/psum | solution.py:207
  (52 shorter events, 0.8 us)
Async XLA Ops:
  6.5 237.8 %copy-start = (bf16[2048,64]{0,1:T(8,128)(2,1)S(1)}, bf16[2048,64]{0,1:T(8,128)(2,1)}, u32[]{:S(2)}) copy-start(bf16[2048,64]{0,1:T(8,128)(2,1)} %param.36) | copy-start | bytes 786436
  6.5 12.8 %copy-start.4 = (s32[8]{0:T(128)S(1)}, s32[8]{0:T(128)}, u32[]{:S(2)}) copy-start(s32[8]{0:T(128)} %param.29) | copy-start | bytes 100
  6.5 14.1 %copy-start.6 = (s32[8]{0:T(128)S(1)}, s32[8]{0:T(128)}, u32[]{:S(2)}) copy-start(s32[8]{0:T(128)} %param.27) | copy-start | bytes 100
  6.5 54.7 %all-gather.6.cloned.1.call-start = ((), (), s32[]{:S(2)}) async-start(), calls=%async_computation.3 | async-start | bytes 2359296 | tf_op jit(solution)/shard_map/all_gather | solution.py:163
  7.3 127.5 %all-gather.8.cloned.1.call-start = ((), (), s32[]{:S(2)}) async-start(), calls=%async_computation.4 | async-start | bytes 4718592 | tf_op jit(solution)/shard_map/all_gather | solution.py:162
  8.0 200.2 %all-gather.4.cloned.1.call-start = ((), (), s32[]{:S(2)}) async-start(), calls=%async_computation.2 | async-start | bytes 4718592 | tf_op jit(solution)/shard_map/all_gather | solution.py:161
  65.6 74.3 %copy-start.7 = (bf16[64,256]{1,0:T(8,128)(2,1)S(1)}, bf16[64,256]{1,0:T(8,128)(2,1)}, u32[]{:S(2)}) copy-start(bf16[64,256]{1,0:T(8,128)(2,1)} %param.26) | copy-start | bytes 98308
  140.3 73.2 %copy-start.5 = (bf16[64,256]{1,0:T(8,128)(2,1)S(1)}, bf16[64,256]{1,0:T(8,128)(2,1)}, u32[]{:S(2)}) copy-start(bf16[64,256]{1,0:T(8,128)(2,1)} %param.25) | copy-start | bytes 98308
  140.3 79.3 %copy-start.9 = (bf16[1,256]{1,0:T(2,128)(2,1)S(1)}, bf16[1,256]{1,0:T(2,128)(2,1)}, u32[]{:S(2)}) copy-start(bf16[1,256]{1,0:T(2,128)(2,1)} %param.32) | copy-start | bytes 1540
  140.3 79.4 %copy-start.1 = (bf16[1,256,256]{2,1,0:T(8,128)(2,1)S(1)}, bf16[1,256,256]{2,1,0:T(8,128)(2,1)}, u32[]{:S(2)}) copy-start(bf16[1,256,256]{2,1,0:T(8,128)(2,1)} %param.33) | copy-start | bytes 393220
  140.3 79.5 %copy-start.2 = (bf16[1,256,256]{2,1,0:T(8,128)(2,1)S(1)}, bf16[1,256,256]{2,1,0:T(8,128)(2,1)}, u32[]{:S(2)}) copy-start(bf16[1,256,256]{2,1,0:T(8,128)(2,1)} %param.34) | copy-start | bytes 393220
  140.3 79.5 %copy-start.8 = (bf16[1,2048]{1,0:T(2,128)(2,1)S(1)}, bf16[1,2048]{1,0:T(2,128)(2,1)}, u32[]{:S(2)}) copy-start(bf16[1,2048]{1,0:T(2,128)(2,1)} %param.30) | copy-start | bytes 12292
  140.3 79.5 %copy-start.10 = (bf16[1,256]{1,0:T(2,128)(2,1)S(1)}, bf16[1,256]{1,0:T(2,128)(2,1)}, u32[]{:S(2)}) copy-start(bf16[1,256]{1,0:T(2,128)(2,1)} %param.31) | copy-start | bytes 1540
  214.0 30.5 %copy-start.3 = (bf16[64,1024]{1,0:T(8,128)(2,1)S(1)}, bf16[64,1024]{1,0:T(8,128)(2,1)}, u32[]{:S(2)}) copy-start(bf16[64,1024]{1,0:T(8,128)(2,1)} %param.37) | copy-start | bytes 393220
  216.2 12.0 %all-to-all-start = ((bf16[8,32,512]{2,1,0:T(8,128)(2,1)}), bf16[8,32,512]{2,1,0:T(8,128)(2,1)S(1)}, u32[]{:S(2)}, u32[]{:S(2)}) async-start(bf16[8,32,512]{2,1,0:T(8,128)(2,1)} %bitcast.24), calls=%async_computation | async-start | bytes 524288 | tf_op jit(solution)/shard_map/all_to_all | solution.py:181
  231.2 10.3 %all-to-all-start.1 = ((bf16[8,2,1024]{2,1,0:T(2,128)(2,1)}), bf16[8,2,1024]{2,1,0:T(2,128)(2,1)S(1)}, u32[]{:S(2)}, u32[]{:S(2)}) async-start(bf16[8,2,1024]{2,1,0:T(2,128)(2,1)} %reshape.379), calls=%async_computation.1 | async-start | bytes 65536 | tf_op jit(solution)/shard_map/all_to_all | solution.py:200
Sparse Core Ops, SparseCore 0:
  9.5 51.7 all-gather.5
  63.4 71.3 all-gather.7
  136.9 71.3 all-gather.3
